TPU v7x, 128 devices: a whole 4x4x4 slice. The times are simulated.
128 devices in a mesh: dp: 8 (over x, core), seq: 16 (over y, z).
Axes of the slice: x: 4, y: 4, z: 4, core: 2. Of those that a mesh axis runs over, the one named last changes fastest.
Arguments:
- queries: bfloat16 [16, 98304, 128], P(None, ('dp', 'seq')), parts along dimension 1, may hold values from -6 to 6
- key_rows: bfloat16 [16, 98304, 128], P(None, ('dp', 'seq')), parts along dimension 1, may hold values from -6 to 6
- value_rows: bfloat16 [16, 98304, 128], P(None, ('dp', 'seq')), parts along dimension 1, may hold values from -6 to 6
- out_grad: bfloat16 [16, 98304, 128], P(None, ('dp', 'seq')), parts along dimension 1, may hold values from -6 to 6
Outputs:
- attended: bfloat16 [16, 98304, 128], P(None, ('dp', 'seq')), parts along dimension 1
- grad_queries: bfloat16 [16, 98304, 128], P(None, ('dp', 'seq')), parts along dimension 1
- grad_keys: bfloat16 [16, 98304, 128], P(None, ('dp', 'seq')), parts along dimension 1
- grad_values: bfloat16 [16, 98304, 128], P(None, ('dp', 'seq')), parts along dimension 1
There are 8 independent parts, one for each index of `dp`. A program takes and returns all parts, laid end to end along the dimension named above; each array names one. Nothing has to cross between parts.
All inputs are finite; a program needn't handle non-finite values.
Results may differ from a plain program's by a relative error of at most 0.009.
Values may be sent and summed in bfloat16 or wider, within the bound.
A program may use at most 192 MiB of HBM per device.

v0:
```python
import jax
import jax.numpy as jnp
from jax import lax
from jax.sharding import PartitionSpec as P


def group_terms(pieces):
    q_blk, k_blk, v_blk, g_blk, pre_blk, suf_blk = pieces
    wide = jnp.float32
    length = q_blk.shape[1]
    rows_idx = jnp.arange(length, dtype=jnp.int32)
    causal = rows_idx[:, None] >= rows_idx[None, :]
    scores = jnp.einsum("htd,hsd->hts", q_blk, k_blk, preferred_element_type=wide)
    masked = jnp.where(causal[None], scores, 0.0).astype(jnp.bfloat16)
    dots = jnp.einsum("htd,hsd->hts", g_blk, v_blk, preferred_element_type=wide)
    mdots = jnp.where(causal[None], dots, 0.0).astype(jnp.bfloat16)
    inner = jnp.einsum("hts,hsd->htd", masked, v_blk, preferred_element_type=wide) + jnp.einsum(
        "hta,hab->htb", q_blk, pre_blk, preferred_element_type=wide
    )
    dq_full = jnp.einsum("hts,hsd->htd", mdots, k_blk, preferred_element_type=wide) + jnp.einsum(
        "htb,hab->hta", g_blk, pre_blk, preferred_element_type=wide
    )
    dk_full = jnp.einsum("hts,htd->hsd", mdots, q_blk, preferred_element_type=wide) + jnp.einsum(
        "hsb,hab->hsa", v_blk, suf_blk, preferred_element_type=wide
    )
    dv_full = jnp.einsum("hts,htd->hsd", masked, g_blk, preferred_element_type=wide) + jnp.einsum(
        "hsa,hab->hsb", k_blk, suf_blk, preferred_element_type=wide
    )
    return (
        inner,
        dq_full.astype(jnp.bfloat16),
        dk_full.astype(jnp.bfloat16),
        dv_full.astype(jnp.bfloat16),
    )


def on_device(queries, key_rows, value_rows, out_grad):
    wide = jnp.float32
    heads, length, width = queries.shape
    my_index = lax.axis_index("seq")
    count = lax.axis_size("seq")
    position = (my_index * length + jnp.arange(length, dtype=jnp.int32)).astype(wide)
    scale = 1.0 / jnp.sqrt(width * (position + 1.0))
    scaled_grad = (scale[None, :, None] * out_grad.astype(wide)).astype(jnp.bfloat16)
    key_state = jnp.einsum(
        "hta,htb->hab", key_rows, value_rows, preferred_element_type=wide
    ).astype(jnp.bfloat16)
    grad_state = jnp.einsum(
        "hta,htb->hab", queries, scaled_grad, preferred_element_type=wide
    ).astype(jnp.bfloat16)
    ranks = jnp.arange(count, dtype=jnp.int32)
    earlier = (ranks < my_index).astype(jnp.bfloat16)
    later = (ranks > my_index).astype(jnp.bfloat16)
    all_keys = lax.all_gather(key_state[None], "seq", axis=0, tiled=True)
    prefix = jnp.einsum("n,nhab->hab", earlier, all_keys, preferred_element_type=wide)
    all_grads = lax.all_gather(grad_state[None], "seq", axis=0, tiled=True)
    suffix = jnp.einsum("n,nhab->hab", later, all_grads, preferred_element_type=wide)
    prefix_half = prefix.astype(jnp.bfloat16)
    suffix_half = suffix.astype(jnp.bfloat16)
    group = 4
    steps_count = heads // group

    def grouped(array):
        return array.reshape((steps_count, group) + array.shape[1:])

    inner, grad_q, grad_k, grad_v = lax.map(
        group_terms,
        (
            grouped(queries),
            grouped(key_rows),
            grouped(value_rows),
            grouped(scaled_grad),
            grouped(prefix_half),
            grouped(suffix_half),
        ),
    )
    attended = (scale[None, :, None] * inner.reshape(heads, length, width)).astype(jnp.bfloat16)
    return (
        attended,
        grad_q.reshape(heads, length, width),
        grad_k.reshape(heads, length, width),
        grad_v.reshape(heads, length, width),
    )


def solution(mesh):
    placed = (
        P(None, ("dp", "seq"), None),
        P(None, ("dp", "seq"), None),
        P(None, ("dp", "seq"), None),
        P(None, ("dp", "seq"), None),
    )
    return jax.shard_map(
        on_device,
        mesh=mesh,
        in_specs=placed,
        out_specs=(
            P(None, ("dp", "seq"), None),
            P(None, ("dp", "seq"), None),
            P(None, ("dp", "seq"), None),
            P(None, ("dp", "seq"), None),
        ),
        check_vma=False,
    )
```

profile of v0, /device:TPU:1, one launch (start us, length us, event | category | flops | bytes accessed | tf_op | source)
XLA Modules:
  0.0 249.8 jit_solution(6098355292058006964)
XLA Ops:
  7.2 4.7 %convolution_convert_fusion.1 = bf16[16,128,128]{2,1,0:T(8,128)(2,1)} fusion(bf16[16,768,128]{2,1,0:T(8,128)(2,1)} %param.7, bf16[16,768,128]{2,1,0:T(8,128)(2,1)} %param.8), kind=kOutput, calls=%fused_computation.67 | convolution fusion | flops 402915328 | bytes 6815744 | tf_op jit(solution)/shard_map/hta,htb->hab/dot_general | solution.py:45
  12.0 2.9 %multiply_convert_fusion = bf16[16,768,128]{2,1,0:T(8,128)(2,1)S(1)} fusion(bf16[16,768,128]{2,1,0:T(8,128)(2,1)} %param.9, f32[768]{0:T(1024)S(1)} %multiply_rsqrt_fusion), kind=kLoop, calls=%fused_computation.65 | loop fusion | flops 4718592 | bytes 6294528 | tf_op jit(solution)/shard_map/convert_element_type | solution.py:44
  15.0 1.9 fusion.57
  16.9 2.1 copy.16
  19.0 67.1 %all-gather.5.cloned.1.call-done = bf16[256,128,128]{2,1,0:T(8,128)(2,1)} async-done(((bf16[16,128,128]{2,1,0:T(8,128)(2,1)}), bf16[256,128,128]{2,1,0:T(8,128)(2,1)}) %all-gather.5.cloned.1.call-update) | async-done | bytes 8388624 | tf_op jit(solution)/shard_map/all_gather | solution.py:54
  86.1 8.3 %fusion.54 = f32[1,16,128,128]{3,0,2,1:T(1,128)S(1)} fusion(bf16[16,16,128,128]{3,2,1,0:T(8,128)(2,1)} %bitcast.143, s32[]{:T(128)S(6)} %axis_index.12), kind=kOutput, calls=%fused_computation.61 | convolution fusion | flops 8388624 | bytes 9437188 | tf_op jit(solution)/shard_map/n,nhab->hab/dot_general | solution.py:55
  95.2 63.5 %all-gather.7.cloned.1.call-done = bf16[256,128,128]{2,1,0:T(8,128)(2,1)} async-done(((bf16[16,128,128]{2,1,0:T(8,128)(2,1)}), bf16[256,128,128]{2,1,0:T(8,128)(2,1)}) %all-gather.7.cloned.1.call-update) | async-done | bytes 8388624 | tf_op jit(solution)/shard_map/all_gather | solution.py:56
  158.7 8.5 %fusion.52 = f32[1,16,128,128]{3,0,2,1:T(1,128)S(1)} fusion(bf16[16,16,128,128]{3,2,1,0:T(8,128)(2,1)} %bitcast.144, s32[]{:T(128)S(6)} %axis_index.12), kind=kOutput, calls=%fused_computation.59 | convolution fusion | flops 8388624 | bytes 9437188 | tf_op jit(solution)/shard_map/n,nhab->hab/dot_general | solution.py:57
  168.1 69.6 %while.16 = (s32[]{:T(128)}, f32[4,4,768,128]{3,2,1,0:T(8,128)}, bf16[4,4,768,128]{3,2,1,0:T(8,128)(2,1)}, bf16[4,4,768,128]{3,2,1,0:T(8,128)(2,1)}, bf16[4,4,76...) while((s32[]{:T(128)}, f32[4,4,768,128]{3,2,1,0:T(8,128)}, ...), condition=%wide.region_1.2_spmd, body=%wide.region_0.1_spmd.sunk | while | flops 4039311360 | bytes 96413928 | solution.py:66
  168.3 1.7 fusion.124
  173.9 2.6 %fusion.125 = bf16[4,4,768,128]{3,2,1,0:T(8,128)(2,1)} fusion(bf16[4,4,768,128]{3,2,1,0:T(8,128)(2,1)} %get-tuple-element.172, s32[]{:T(128)S(6)} %copy.40, f32[4,768,128]{2,1,0:T(8,128)S(1)} %fusion.124, bf16[4,768,768]{2,1,0:T(8,128)(2,1)S(1)} %select_convert_fusion.5, bf16[4,4,768,128]{3,2,1,0:T(8,128)(2,1)S(1)} %copy-done.1), kind=kOutput, calls=%fused_computation.10.clone.1 | convolution fusion | flops 604766208 | bytes 7865344 | tf_op jit(solution)/shard_map/while/body/eval_jaxpr/hts,htd->hsd/dot_general | solution.py:23
  176.5 2.3 fusion.123
  180.3 2.6 %fusion.127 = bf16[4,4,768,128]{3,2,1,0:T(8,128)(2,1)} fusion(bf16[4,4,768,128]{3,2,1,0:T(8,128)(2,1)} %get-tuple-element.173, s32[]{:T(128)S(6)} %copy.40, f32[4,768,128]{2,1,0:T(8,128)S(1)} %fusion.126, bf16[4,768,768]{2,1,0:T(8,128)(2,1)S(1)} %select_convert_fusion.4, bf16[4,4,768,128]{3,2,1,0:T(8,128)(2,1)S(1)} %get-tuple-element.190), kind=kOutput, calls=%fused_computation.12.clone.1 | convolution fusion | flops 604766208 | bytes 7865344 | tf_op jit(solution)/shard_map/while/body/eval_jaxpr/hts,htd->hsd/dot_general | solution.py:26
  182.9 2.6 %bitcast_dynamic-update-slice_fusion.2 = f32[4,4,768,128]{3,2,1,0:T(8,128)} fusion(f32[4,4,768,128]{3,2,1,0:T(8,128)} %get-tuple-element.170, s32[]{:T(128)S(6)} %copy.40, f32[4,768,128]{2,1,0:T(8,128)S(1)} %fusion.121, bf16[4,768,768]{2,1,0:T(8,128)(2,1)S(1)} %select_convert_fusion.4, bf16[4,4,768,128]{3,2,1,0:T(8,128)(2,1)S(1)} %copy-done.2), kind=kOutput, calls=%fused_computation.3.clone.1 | convolution fusion | flops 604372992 | bytes 8651776 | tf_op jit(solution)/shard_map/while/body/eval_jaxpr/hts,hsd->htd/dot_general | solution.py:17
  185.7 1.7 fusion.124
  187.4 1.6 fusion.126
  191.3 2.6 %fusion.125 = bf16[4,4,768,128]{3,2,1,0:T(8,128)(2,1)} fusion(bf16[4,4,768,128]{3,2,1,0:T(8,128)(2,1)} %get-tuple-element.172, s32[]{:T(128)S(6)} %copy.40, f32[4,768,128]{2,1,0:T(8,128)S(1)} %fusion.124, bf16[4,768,768]{2,1,0:T(8,128)(2,1)S(1)} %select_convert_fusion.5, bf16[4,4,768,128]{3,2,1,0:T(8,128)(2,1)S(1)} %copy-done.1), kind=kOutput, calls=%fused_computation.10.clone.1 | convolution fusion | flops 604766208 | bytes 7865344 | tf_op jit(solution)/shard_map/while/body/eval_jaxpr/hts,htd->hsd/dot_general | solution.py:23
  193.9 2.3 fusion.123
  197.7 2.6 %fusion.127 = bf16[4,4,768,128]{3,2,1,0:T(8,128)(2,1)} fusion(bf16[4,4,768,128]{3,2,1,0:T(8,128)(2,1)} %get-tuple-element.173, s32[]{:T(128)S(6)} %copy.40, f32[4,768,128]{2,1,0:T(8,128)S(1)} %fusion.126, bf16[4,768,768]{2,1,0:T(8,128)(2,1)S(1)} %select_convert_fusion.4, bf16[4,4,768,128]{3,2,1,0:T(8,128)(2,1)S(1)} %get-tuple-element.190), kind=kOutput, calls=%fused_computation.12.clone.1 | convolution fusion | flops 604766208 | bytes 7865344 | tf_op jit(solution)/shard_map/while/body/eval_jaxpr/hts,htd->hsd/dot_general | solution.py:26
  200.3 2.6 %bitcast_dynamic-update-slice_fusion.2 = f32[4,4,768,128]{3,2,1,0:T(8,128)} fusion(f32[4,4,768,128]{3,2,1,0:T(8,128)} %get-tuple-element.170, s32[]{:T(128)S(6)} %copy.40, f32[4,768,128]{2,1,0:T(8,128)S(1)} %fusion.121, bf16[4,768,768]{2,1,0:T(8,128)(2,1)S(1)} %select_convert_fusion.4, bf16[4,4,768,128]{3,2,1,0:T(8,128)(2,1)S(1)} %copy-done.2), kind=kOutput, calls=%fused_computation.3.clone.1 | convolution fusion | flops 604372992 | bytes 8651776 | tf_op jit(solution)/shard_map/while/body/eval_jaxpr/hts,hsd->htd/dot_general | solution.py:17
  203.1 1.7 fusion.124
  204.7 1.6 fusion.126
  208.7 2.6 %fusion.125 = bf16[4,4,768,128]{3,2,1,0:T(8,128)(2,1)} fusion(bf16[4,4,768,128]{3,2,1,0:T(8,128)(2,1)} %get-tuple-element.172, s32[]{:T(128)S(6)} %copy.40, f32[4,768,128]{2,1,0:T(8,128)S(1)} %fusion.124, bf16[4,768,768]{2,1,0:T(8,128)(2,1)S(1)} %select_convert_fusion.5, bf16[4,4,768,128]{3,2,1,0:T(8,128)(2,1)S(1)} %copy-done.1), kind=kOutput, calls=%fused_computation.10.clone.1 | convolution fusion | flops 604766208 | bytes 7865344 | tf_op jit(solution)/shard_map/while/body/eval_jaxpr/hts,htd->hsd/dot_general | solution.py:23
  211.3 2.3 fusion.123
  215.1 2.6 %fusion.127 = bf16[4,4,768,128]{3,2,1,0:T(8,128)(2,1)} fusion(bf16[4,4,768,128]{3,2,1,0:T(8,128)(2,1)} %get-tuple-element.173, s32[]{:T(128)S(6)} %copy.40, f32[4,768,128]{2,1,0:T(8,128)S(1)} %fusion.126, bf16[4,768,768]{2,1,0:T(8,128)(2,1)S(1)} %select_convert_fusion.4, bf16[4,4,768,128]{3,2,1,0:T(8,128)(2,1)S(1)} %get-tuple-element.190), kind=kOutput, calls=%fused_computation.12.clone.1 | convolution fusion | flops 604766208 | bytes 7865344 | tf_op jit(solution)/shard_map/while/body/eval_jaxpr/hts,htd->hsd/dot_general | solution.py:26
  217.7 2.6 %bitcast_dynamic-update-slice_fusion.2 = f32[4,4,768,128]{3,2,1,0:T(8,128)} fusion(f32[4,4,768,128]{3,2,1,0:T(8,128)} %get-tuple-element.170, s32[]{:T(128)S(6)} %copy.40, f32[4,768,128]{2,1,0:T(8,128)S(1)} %fusion.121, bf16[4,768,768]{2,1,0:T(8,128)(2,1)S(1)} %select_convert_fusion.4, bf16[4,4,768,128]{3,2,1,0:T(8,128)(2,1)S(1)} %copy-done.2), kind=kOutput, calls=%fused_computation.3.clone.1 | convolution fusion | flops 604372992 | bytes 8651776 | tf_op jit(solution)/shard_map/while/body/eval_jaxpr/hts,hsd->htd/dot_general | solution.py:17
  220.5 1.7 fusion.124
  226.1 2.6 %fusion.125 = bf16[4,4,768,128]{3,2,1,0:T(8,128)(2,1)} fusion(bf16[4,4,768,128]{3,2,1,0:T(8,128)(2,1)} %get-tuple-element.172, s32[]{:T(128)S(6)} %copy.40, f32[4,768,128]{2,1,0:T(8,128)S(1)} %fusion.124, bf16[4,768,768]{2,1,0:T(8,128)(2,1)S(1)} %select_convert_fusion.5, bf16[4,4,768,128]{3,2,1,0:T(8,128)(2,1)S(1)} %copy-done.1), kind=kOutput, calls=%fused_computation.10.clone.1 | convolution fusion | flops 604766208 | bytes 7865344 | tf_op jit(solution)/shard_map/while/body/eval_jaxpr/hts,htd->hsd/dot_general | solution.py:23
  228.7 2.3 fusion.123
  232.5 2.6 %fusion.127 = bf16[4,4,768,128]{3,2,1,0:T(8,128)(2,1)} fusion(bf16[4,4,768,128]{3,2,1,0:T(8,128)(2,1)} %get-tuple-element.173, s32[]{:T(128)S(6)} %copy.40, f32[4,768,128]{2,1,0:T(8,128)S(1)} %fusion.126, bf16[4,768,768]{2,1,0:T(8,128)(2,1)S(1)} %select_convert_fusion.4, bf16[4,4,768,128]{3,2,1,0:T(8,128)(2,1)S(1)} %get-tuple-element.190), kind=kOutput, calls=%fused_computation.12.clone.1 | convolution fusion | flops 604766208 | bytes 7865344 | tf_op jit(solution)/shard_map/while/body/eval_jaxpr/hts,htd->hsd/dot_general | solution.py:26
  235.1 2.6 %bitcast_dynamic-update-slice_fusion.2 = f32[4,4,768,128]{3,2,1,0:T(8,128)} fusion(f32[4,4,768,128]{3,2,1,0:T(8,128)} %get-tuple-element.170, s32[]{:T(128)S(6)} %copy.40, f32[4,768,128]{2,1,0:T(8,128)S(1)} %fusion.121, bf16[4,768,768]{2,1,0:T(8,128)(2,1)S(1)} %select_convert_fusion.4, bf16[4,4,768,128]{3,2,1,0:T(8,128)(2,1)S(1)} %copy-done.2), kind=kOutput, calls=%fused_computation.3.clone.1 | convolution fusion | flops 604372992 | bytes 8651776 | tf_op jit(solution)/shard_map/while/body/eval_jaxpr/hts,hsd->htd/dot_general | solution.py:17
  237.7 5.2 %fusion.56 = bf16[16,768,128]{2,1,0:T(8,128)(2,1)} fusion(f32[4,4,768,128]{3,2,1,0:T(8,128)} %get-tuple-element.64, f32[768]{0:T(1024)S(1)} %multiply_rsqrt_fusion), kind=kLoop, calls=%fused_computation.64 | loop fusion | flops 3145728 | bytes 9440256 | tf_op jit(solution)/shard_map/convert_element_type | solution.py:77
  (67 shorter events, 20.8 us)
Async XLA Ops:
  7.2 78.9 %all-gather.5.cloned.1.call-start = ((), (), s32[]{:S(2)}) async-start(), calls=%async_computation | async-start | bytes 8912896 | tf_op jit(solution)/shard_map/all_gather | solution.py:54
  11.9 146.8 %all-gather.7.cloned.1.call-start = ((), (), s32[]{:S(2)}) async-start(), calls=%async_computation.1 | async-start | bytes 8912896 | tf_op jit(solution)/shard_map/all_gather | solution.py:56
  12.0 3.0 %copy-start = (bf16[16,768,128]{2,1,0:T(8,128)(2,1)S(1)}, bf16[16,768,128]{2,1,0:T(8,128)(2,1)}, u32[]{:S(2)}) copy-start(bf16[16,768,128]{2,1,0:T(8,128)(2,1)} %param.6) | copy-start | bytes 9437188
  168.1 3.5 %copy-start.1 = (bf16[4,4,768,128]{3,2,1,0:T(8,128)(2,1)S(1)}, bf16[4,4,768,128]{3,2,1,0:T(8,128)(2,1)}, u32[]{:S(2)}) copy-start(bf16[4,4,768,128]{3,2,1,0:T(8,128)(2,1)} %get-tuple-element.186) | copy-start | bytes 9437188 | tf_op jit(solution)/shard_map/while
  168.1 3.5 %copy-start.4 = (bf16[4,4,128,128]{3,2,1,0:T(8,128)(2,1)S(1)}, bf16[4,4,128,128]{3,2,1,0:T(8,128)(2,1)}, u32[]{:S(2)}) copy-start(bf16[4,4,128,128]{3,2,1,0:T(8,128)(2,1)} %get-tuple-element.189) | copy-start | bytes 1572868 | tf_op jit(solution)/shard_map/while
  170.0 2.4 copy-start.2
  173.9 2.6 %copy-start.3 = (bf16[4,4,768,128]{3,2,1,0:T(8,128)(2,1)S(1)}, bf16[4,4,768,128]{3,2,1,0:T(8,128)(2,1)}, u32[]{:S(2)}) copy-start(bf16[4,4,768,128]{3,2,1,0:T(8,128)(2,1)} %get-tuple-element.187) | copy-start | bytes 9437188 | tf_op jit(solution)/shard_map/while
  185.5 3.5 %copy-start.1 = (bf16[4,4,768,128]{3,2,1,0:T(8,128)(2,1)S(1)}, bf16[4,4,768,128]{3,2,1,0:T(8,128)(2,1)}, u32[]{:S(2)}) copy-start(bf16[4,4,768,128]{3,2,1,0:T(8,128)(2,1)} %get-tuple-element.186) | copy-start | bytes 9437188 | tf_op jit(solution)/shard_map/while
  185.5 3.5 %copy-start.4 = (bf16[4,4,128,128]{3,2,1,0:T(8,128)(2,1)S(1)}, bf16[4,4,128,128]{3,2,1,0:T(8,128)(2,1)}, u32[]{:S(2)}) copy-start(bf16[4,4,128,128]{3,2,1,0:T(8,128)(2,1)} %get-tuple-element.189) | copy-start | bytes 1572868 | tf_op jit(solution)/shard_map/while
  187.3 2.4 copy-start.2
  191.3 2.6 %copy-start.3 = (bf16[4,4,768,128]{3,2,1,0:T(8,128)(2,1)S(1)}, bf16[4,4,768,128]{3,2,1,0:T(8,128)(2,1)}, u32[]{:S(2)}) copy-start(bf16[4,4,768,128]{3,2,1,0:T(8,128)(2,1)} %get-tuple-element.187) | copy-start | bytes 9437188 | tf_op jit(solution)/shard_map/while
  202.9 3.5 %copy-start.1 = (bf16[4,4,768,128]{3,2,1,0:T(8,128)(2,1)S(1)}, bf16[4,4,768,128]{3,2,1,0:T(8,128)(2,1)}, u32[]{:S(2)}) copy-start(bf16[4,4,768,128]{3,2,1,0:T(8,128)(2,1)} %get-tuple-element.186) | copy-start | bytes 9437188 | tf_op jit(solution)/shard_map/while
  202.9 3.5 %copy-start.4 = (bf16[4,4,128,128]{3,2,1,0:T(8,128)(2,1)S(1)}, bf16[4,4,128,128]{3,2,1,0:T(8,128)(2,1)}, u32[]{:S(2)}) copy-start(bf16[4,4,128,128]{3,2,1,0:T(8,128)(2,1)} %get-tuple-element.189) | copy-start | bytes 1572868 | tf_op jit(solution)/shard_map/while
  204.7 2.4 copy-start.2
  208.7 2.6 %copy-start.3 = (bf16[4,4,768,128]{3,2,1,0:T(8,128)(2,1)S(1)}, bf16[4,4,768,128]{3,2,1,0:T(8,128)(2,1)}, u32[]{:S(2)}) copy-start(bf16[4,4,768,128]{3,2,1,0:T(8,128)(2,1)} %get-tuple-element.187) | copy-start | bytes 9437188 | tf_op jit(solution)/shard_map/while
  220.3 3.5 %copy-start.1 = (bf16[4,4,768,128]{3,2,1,0:T(8,128)(2,1)S(1)}, bf16[4,4,768,128]{3,2,1,0:T(8,128)(2,1)}, u32[]{:S(2)}) copy-start(bf16[4,4,768,128]{3,2,1,0:T(8,128)(2,1)} %get-tuple-element.186) | copy-start | bytes 9437188 | tf_op jit(solution)/shard_map/while
  220.3 3.5 %copy-start.4 = (bf16[4,4,128,128]{3,2,1,0:T(8,128)(2,1)S(1)}, bf16[4,4,128,128]{3,2,1,0:T(8,128)(2,1)}, u32[]{:S(2)}) copy-start(bf16[4,4,128,128]{3,2,1,0:T(8,128)(2,1)} %get-tuple-element.189) | copy-start | bytes 1572868 | tf_op jit(solution)/shard_map/while
  222.1 2.4 copy-start.2
  226.1 2.6 %copy-start.3 = (bf16[4,4,768,128]{3,2,1,0:T(8,128)(2,1)S(1)}, bf16[4,4,768,128]{3,2,1,0:T(8,128)(2,1)}, u32[]{:S(2)}) copy-start(bf16[4,4,768,128]{3,2,1,0:T(8,128)(2,1)} %get-tuple-element.187) | copy-start | bytes 9437188 | tf_op jit(solution)/shard_map/while
Sparse Core Ops, SparseCore 0:
  12.1 73.9 all-gather.4
  88.2 70.4 all-gather.6
where the time goes:
time: 250 us
  waiting for transfers between devices  131 us (52%)
  matrix products  91.8 us (37%)
  between operations  14.1 us (6%)
  other arithmetic  10.7 us (4%)
    all_gather x1, waiting for transfers between devices, on_device(): all_keys = lax.all_gather(key_state[None], 'seq', axis=0, tiled=True)  67.1 us
    all_gather x1, waiting for transfers between devices, on_device(): all_grads = lax.all_gather(grad_state[None], 'seq', axis=0, tiled=True)  63.5 us
    dot_general x4, matrix products, group_terms(): jnp.einsum('hts,htd->hsd', masked, g_blk, preferred_element_type=wide)  10.5 us
    dot_general x4, matrix products, group_terms(): jnp.einsum('hts,htd->hsd', mdots, q_blk, preferred_element_type=wide)  10.4 us
    dot_general x4, matrix products, group_terms(): jnp.einsum('hts,hsd->htd', masked, v_blk, preferred_element_type=wide)  10.3 us
    dot_general x4, matrix products, group_terms(): jnp.einsum('hts,hsd->htd', mdots, k_blk, preferred_element_type=wide)  9.14 us
    dot_general x1, matrix products, on_device(): jnp.einsum('n,nhab->hab', later, all_grads, preferred_element_type=wide)  8.47 us
    dot_general x1, matrix products, on_device(): jnp.einsum('n,nhab->hab', earlier, all_keys, preferred_element_type=wide)  8.3 us
  transfers between devices with their start and end apart: 2, of which 2 were waited for; matrix products, arithmetic and copies ran while one was open for 6% of the time, Pallas kernels for 0%

commit v1 on v0

--- a/solution.py
+++ b/solution.py
@@ -35,6 +35,19 @@
 
 
 def on_device(queries, key_rows, value_rows, out_grad):
+
+    def bind_pools(xs):
+        n_now = jnp.concatenate(
+            lax.all_to_all(
+                jnp.stack([xs for _ in range(lax.axis_size("seq"))], axis=0),
+                concat_axis=0,
+                split_axis=0,
+                axis_name="seq",
+            ),
+            axis=0,
+        )
+        return n_now
+
     wide = jnp.float32
     heads, length, width = queries.shape
     my_index = lax.axis_index("seq")
@@ -53,7 +66,7 @@
     later = (ranks > my_index).astype(jnp.bfloat16)
     all_keys = lax.all_gather(key_state[None], "seq", axis=0, tiled=True)
     prefix = jnp.einsum("n,nhab->hab", earlier, all_keys, preferred_element_type=wide)
-    all_grads = lax.all_gather(grad_state[None], "seq", axis=0, tiled=True)
+    all_grads = bind_pools(grad_state[None])
     suffix = jnp.einsum("n,nhab->hab", later, all_grads, preferred_element_type=wide)
     prefix_half = prefix.astype(jnp.bfloat16)
     suffix_half = suffix.astype(jnp.bfloat16)

time: 250 us -> 293 us (1.17)
  waiting for transfers between devices: 131 us -> 162 us
  starting transfers between devices: 0.08 us -> 8.75 us
  local copies, waits for them, and re-layouts: 2.15 us -> 8.88 us
  matrix products: 91.8 us -> 87.8 us
    all_to_all x0 -> x1, waiting for transfers between devices: none -> 162 us  [bind_pools(): lax.all_to_all(jnp.stack([xs for _ in range(lax.axis_size('seq'))], axis=...]
    all_gather x1, waiting for transfers between devices: 67.1 us -> 0.01 us  [on_device(): all_keys = lax.all_gather(key_state[None], 'seq', axis=0, tiled=True)]
    all_gather x1 -> x0, waiting for transfers between devices: 63.5 us -> none  [on_device(): all_grads = lax.all_gather(grad_state[None], 'seq', axis=0, tiled=True)]
    all_to_all x0 -> x1, starting transfers between devices: none -> 8.71 us  [bind_pools(): lax.all_to_all(jnp.stack([xs for _ in range(lax.axis_size('seq'))], axis=...]
    another operation x0 -> x1, local copies, waits for them, and re-layouts: none -> 6.39 us  [bind_pools(): jnp.stack([xs for _ in range(lax.axis_size('seq'))], axis=0)]
    dot_general x4, matrix products: 5.96 us -> 12 us  [group_terms(): jnp.einsum('htd,hsd->hts', q_blk, k_blk, preferred_element_type=wide)]
    dot_general x4, matrix products: 6.59 us -> 1.39 us  [group_terms(): jnp.einsum('hsa,hab->hsb', k_blk, suf_blk, preferred_element_type=wide)]
    dot_general x4, matrix products: 6.64 us -> 1.47 us  [group_terms(): jnp.einsum('hsb,hab->hsa', v_blk, suf_blk, preferred_element_type=wide)]
  transfers between devices with their start and end apart: 2 -> 2, of which waited for: 2 -> 1; matrix products, arithmetic and copies ran while one was open for 6% -> 8% of each run, Pallas kernels for 0% -> 0%
where the time goes in v1:
time: 293 us; the launch traced here: 292 us
  waiting for transfers between devices  162 us (55%)
  matrix products  87.8 us (30%)
  between operations  14.1 us (5%)
  other arithmetic  10.7 us (4%)
  local copies, waits for them, and re-layouts  8.88 us (3%)
  starting transfers between devices  8.75 us (3%)
    all_to_all x1, waiting for transfers between devices, bind_pools(): lax.all_to_all(jnp.stack([xs for _ in range(lax.axis_size('seq'))], axis=...  162 us
    dot_general x4, matrix products, group_terms(): jnp.einsum('htd,hsd->hts', q_blk, k_blk, preferred_element_type=wide)  12 us
    dot_general x4, matrix products, group_terms(): jnp.einsum('hts,hsd->htd', masked, v_blk, preferred_element_type=wide)  10.6 us
    dot_general x4, matrix products, group_terms(): jnp.einsum('hts,htd->hsd', masked, g_blk, preferred_element_type=wide)  10.5 us
    dot_general x4, matrix products, group_terms(): jnp.einsum('hts,htd->hsd', mdots, q_blk, preferred_element_type=wide)  10.4 us
    dot_general x4, matrix products, group_terms(): jnp.einsum('hts,hsd->htd', mdots, k_blk, preferred_element_type=wide)  9.4 us
    all_to_all x1, starting transfers between devices, bind_pools(): lax.all_to_all(jnp.stack([xs for _ in range(lax.axis_size('seq'))], axis=...  8.71 us
    dot_general x1, matrix products, on_device(): jnp.einsum('n,nhab->hab', earlier, all_keys, preferred_element_type=wide)  8.3 us
  transfers between devices with their start and end apart: 2, of which 1 were waited for; matrix products, arithmetic and copies ran while one was open for 8% of the time, Pallas kernels for 0%

profile of v1, /device:TPU:1, one launch (start us, length us, event | category | flops | bytes accessed | tf_op | source)
XLA Modules:
  0.0 292.5 jit_solution(8878645797561867769)
XLA Ops:
  7.2 4.7 %convolution_convert_fusion.1 = bf16[16,128,128]{2,1,0:T(8,128)(2,1)} fusion(bf16[16,768,128]{2,1,0:T(8,128)(2,1)} %param.7, bf16[16,768,128]{2,1,0:T(8,128)(2,1)} %param.8), kind=kOutput, calls=%fused_computation.67 | convolution fusion | flops 402915328 | bytes 6815744 | tf_op jit(solution)/shard_map/hta,htb->hab/dot_general | solution.py:58
  12.0 2.9 %multiply_convert_fusion = bf16[16,768,128]{2,1,0:T(8,128)(2,1)S(1)} fusion(bf16[16,768,128]{2,1,0:T(8,128)(2,1)} %param.9, f32[768]{0:T(1024)S(1)} %multiply_rsqrt_fusion), kind=kLoop, calls=%fused_computation.65 | loop fusion | flops 4718592 | bytes 6294528 | tf_op jit(solution)/shard_map/convert_element_type | solution.py:57
  14.9 1.9 fusion.57
  16.8 2.0 copy.17
  18.9 6.4 %stack.3 = bf16[16,1,16,128,128]{4,3,2,1,0:T(8,128)(2,1)} broadcast(bf16[16,128,128]{2,1,0:T(8,128)(2,1)} %copy.17), dimensions={2,3,4} | broadcast | bytes 8912896 | tf_op jit(solution)/shard_map/stack | solution.py:42
  25.3 8.7 %all-to-all-start = ((bf16[16,1,16,128,128]{4,3,2,1,0:T(8,128)(2,1)}), bf16[16,1,16,128,128]{4,3,2,1,0:T(8,128)(2,1)}, u32[]{:S(2)}, u32[]{:S(2)}) async-start(bf16[16,1,16,128,128]{4,3,2,1,0:T(8,128)(2,1)} %stack.3), calls=%async_computation | async-start | bytes 16777216 | tf_op jit(solution)/shard_map/all_to_all | solution.py:41
  34.0 161.9 %all-to-all-done = bf16[16,1,16,128,128]{4,3,2,1,0:T(8,128)(2,1)} async-done(((bf16[16,1,16,128,128]{4,3,2,1,0:T(8,128)(2,1)}), bf16[16,1,16,128,128]{4,3,2,1,0:T(8,128)(2,1)}, u32[]{:S(2)}, u32[]{:S(2)}) %all-to-all-start) | async-done | bytes 8388640 | tf_op jit(solution)/shard_map/all_to_all | solution.py:41
  195.9 8.3 %fusion.52 = f32[1,16,128,128]{3,0,2,1:T(1,128)S(1)} fusion(bf16[16,16,128,128]{3,2,1,0:T(8,128)(2,1)} %bitcast.23, s32[]{:T(128)S(6)} %axis_index.12), kind=kOutput, calls=%fused_computation.59 | convolution fusion | flops 8388624 | bytes 9437188 | tf_op jit(solution)/shard_map/n,nhab->hab/dot_general | solution.py:70
  205.1 8.3 %fusion.54 = f32[1,16,128,128]{3,0,2,1:T(1,128)S(1)} fusion(bf16[16,16,128,128]{3,2,1,0:T(8,128)(2,1)} %bitcast.143, s32[]{:T(128)S(6)} %axis_index.12), kind=kOutput, calls=%fused_computation.61 | convolution fusion | flops 8388624 | bytes 9437188 | tf_op jit(solution)/shard_map/n,nhab->hab/dot_general | solution.py:68
  214.3 66.1 %while.16 = (s32[]{:T(128)}, f32[4,4,768,128]{3,2,1,0:T(8,128)}, bf16[4,4,768,128]{3,2,1,0:T(8,128)(2,1)}, bf16[4,4,768,128]{3,2,1,0:T(8,128)(2,1)}, bf16[4,4,76...) while((s32[]{:T(128)}, f32[4,4,768,128]{3,2,1,0:T(8,128)}, ...), condition=%wide.region_1.2_spmd, body=%wide.region_0.1_spmd.sunk | while | flops 4039311360 | bytes 98511104 | solution.py:79
  214.5 3.0 %select_convert_fusion.4 = bf16[4,768,768]{2,1,0:T(8,128)(2,1)S(1)} fusion(pred[768,768]{1,0:T(8,128)(4,1)S(1)} %iota_compare_fusion.2, bf16[4,4,768,128]{3,2,1,0:T(8,128)(2,1)} %get-tuple-element.187, s32[]{:T(128)} %get-tuple-element.169, bf16[4,4,768,128]{3,2,1,0:T(8,128)(2,1)} %get-tuple-element.186), kind=kOutput, calls=%fused_computation.1.clone.1 | convolution fusion | flops 608698368 | bytes 6882304 | tf_op jit(solution)/shard_map/while/body/eval_jaxpr/htd,hsd->hts/dot_general | solution.py:13
  218.0 2.7 bitcast_dynamic-update-slice_fusion.2
  222.5 2.4 fusion.123
  225.2 2.6 fusion.125
  228.2 2.6 fusion.127
  231.0 3.0 %select_convert_fusion.4 = bf16[4,768,768]{2,1,0:T(8,128)(2,1)S(1)} fusion(pred[768,768]{1,0:T(8,128)(4,1)S(1)} %iota_compare_fusion.2, bf16[4,4,768,128]{3,2,1,0:T(8,128)(2,1)} %get-tuple-element.187, s32[]{:T(128)} %get-tuple-element.169, bf16[4,4,768,128]{3,2,1,0:T(8,128)(2,1)} %get-tuple-element.186), kind=kOutput, calls=%fused_computation.1.clone.1 | convolution fusion | flops 608698368 | bytes 6882304 | tf_op jit(solution)/shard_map/while/body/eval_jaxpr/htd,hsd->hts/dot_general | solution.py:13
  234.5 2.6 bitcast_dynamic-update-slice_fusion.2
  237.1 1.5 select_convert_fusion.5
  239.0 2.4 fusion.123
  241.7 2.6 fusion.125
  244.7 2.6 fusion.127
  247.5 3.0 %select_convert_fusion.4 = bf16[4,768,768]{2,1,0:T(8,128)(2,1)S(1)} fusion(pred[768,768]{1,0:T(8,128)(4,1)S(1)} %iota_compare_fusion.2, bf16[4,4,768,128]{3,2,1,0:T(8,128)(2,1)} %get-tuple-element.187, s32[]{:T(128)} %get-tuple-element.169, bf16[4,4,768,128]{3,2,1,0:T(8,128)(2,1)} %get-tuple-element.186), kind=kOutput, calls=%fused_computation.1.clone.1 | convolution fusion | flops 608698368 | bytes 6882304 | tf_op jit(solution)/shard_map/while/body/eval_jaxpr/htd,hsd->hts/dot_general | solution.py:13
  251.0 2.7 bitcast_dynamic-update-slice_fusion.2
  255.6 2.4 fusion.123
  258.3 2.6 fusion.125
  261.2 2.6 fusion.127
  264.1 3.0 %select_convert_fusion.4 = bf16[4,768,768]{2,1,0:T(8,128)(2,1)S(1)} fusion(pred[768,768]{1,0:T(8,128)(4,1)S(1)} %iota_compare_fusion.2, bf16[4,4,768,128]{3,2,1,0:T(8,128)(2,1)} %get-tuple-element.187, s32[]{:T(128)} %get-tuple-element.169, bf16[4,4,768,128]{3,2,1,0:T(8,128)(2,1)} %get-tuple-element.186), kind=kOutput, calls=%fused_computation.1.clone.1 | convolution fusion | flops 608698368 | bytes 6882304 | tf_op jit(solution)/shard_map/while/body/eval_jaxpr/htd,hsd->hts/dot_general | solution.py:13
  267.5 2.6 bitcast_dynamic-update-slice_fusion.2
  272.1 2.4 fusion.123
  274.8 2.6 fusion.125
  277.7 2.6 fusion.127
  280.4 5.2 %fusion.56 = bf16[16,768,128]{2,1,0:T(8,128)(2,1)} fusion(f32[4,4,768,128]{3,2,1,0:T(8,128)} %get-tuple-element.64, f32[768]{0:T(1024)S(1)} %multiply_rsqrt_fusion), kind=kLoop, calls=%fused_computation.64 | loop fusion | flops 3145728 | bytes 9440256 | tf_op jit(solution)/shard_map/convert_element_type | solution.py:90
  (75 shorter events, 13.3 us)
Async XLA Ops:
  7.2 197.9 %all-gather.3.cloned.1.call-start = ((), (), s32[]{:S(2)}) async-start(), calls=%async_computation.1 | async-start | bytes 8912896 | tf_op jit(solution)/shard_map/all_gather | solution.py:67
  12.0 3.0 %copy-start = (bf16[16,768,128]{2,1,0:T(8,128)(2,1)S(1)}, bf16[16,768,128]{2,1,0:T(8,128)(2,1)}, u32[]{:S(2)}) copy-start(bf16[16,768,128]{2,1,0:T(8,128)(2,1)} %param.6) | copy-start | bytes 9437188
  25.3 170.6 %all-to-all-start = ((bf16[16,1,16,128,128]{4,3,2,1,0:T(8,128)(2,1)}), bf16[16,1,16,128,128]{4,3,2,1,0:T(8,128)(2,1)}, u32[]{:S(2)}, u32[]{:S(2)}) async-start(bf16[16,1,16,128,128]{4,3,2,1,0:T(8,128)(2,1)} %stack.3), calls=%async_computation | async-start | bytes 16777216 | tf_op jit(solution)/shard_map/all_to_all | solution.py:41
  214.5 3.0 %copy-start.1 = (bf16[4,4,768,128]{3,2,1,0:T(8,128)(2,1)S(1)}, bf16[4,4,768,128]{3,2,1,0:T(8,128)(2,1)}, u32[]{:S(2)}) copy-start(bf16[4,4,768,128]{3,2,1,0:T(8,128)(2,1)} %get-tuple-element.186) | copy-start | bytes 9437188 | tf_op jit(solution)/shard_map/while
  214.5 3.0 %copy-start.5 = (bf16[4,4,128,128]{3,2,1,0:T(8,128)(2,1)S(1)}, bf16[4,4,128,128]{3,2,1,0:T(8,128)(2,1)}, u32[]{:S(2)}) copy-start(bf16[4,4,128,128]{3,2,1,0:T(8,128)(2,1)} %get-tuple-element.189) | copy-start | bytes 1572868 | tf_op jit(solution)/shard_map/while
  214.5 3.5 %copy-start.2 = (bf16[4,4,768,128]{3,2,1,0:T(8,128)(2,1)S(1)}, bf16[4,4,768,128]{3,2,1,0:T(8,128)(2,1)}, u32[]{:S(2)}) copy-start(bf16[4,4,768,128]{3,2,1,0:T(8,128)(2,1)} %get-tuple-element.188) | copy-start | bytes 9437188 | tf_op jit(solution)/shard_map/while
  220.6 1.9 copy-start.3
  222.5 2.4 copy-start.4
  231.0 3.0 %copy-start.1 = (bf16[4,4,768,128]{3,2,1,0:T(8,128)(2,1)S(1)}, bf16[4,4,768,128]{3,2,1,0:T(8,128)(2,1)}, u32[]{:S(2)}) copy-start(bf16[4,4,768,128]{3,2,1,0:T(8,128)(2,1)} %get-tuple-element.186) | copy-start | bytes 9437188 | tf_op jit(solution)/shard_map/while
  231.0 3.0 %copy-start.5 = (bf16[4,4,128,128]{3,2,1,0:T(8,128)(2,1)S(1)}, bf16[4,4,128,128]{3,2,1,0:T(8,128)(2,1)}, u32[]{:S(2)}) copy-start(bf16[4,4,128,128]{3,2,1,0:T(8,128)(2,1)} %get-tuple-element.189) | copy-start | bytes 1572868 | tf_op jit(solution)/shard_map/while
  231.0 3.5 %copy-start.2 = (bf16[4,4,768,128]{3,2,1,0:T(8,128)(2,1)S(1)}, bf16[4,4,768,128]{3,2,1,0:T(8,128)(2,1)}, u32[]{:S(2)}) copy-start(bf16[4,4,768,128]{3,2,1,0:T(8,128)(2,1)} %get-tuple-element.188) | copy-start | bytes 9437188 | tf_op jit(solution)/shard_map/while
  237.1 1.9 copy-start.3
  239.0 2.4 copy-start.4
  247.5 3.0 %copy-start.1 = (bf16[4,4,768,128]{3,2,1,0:T(8,128)(2,1)S(1)}, bf16[4,4,768,128]{3,2,1,0:T(8,128)(2,1)}, u32[]{:S(2)}) copy-start(bf16[4,4,768,128]{3,2,1,0:T(8,128)(2,1)} %get-tuple-element.186) | copy-start | bytes 9437188 | tf_op jit(solution)/shard_map/while
  247.5 3.0 %copy-start.5 = (bf16[4,4,128,128]{3,2,1,0:T(8,128)(2,1)S(1)}, bf16[4,4,128,128]{3,2,1,0:T(8,128)(2,1)}, u32[]{:S(2)}) copy-start(bf16[4,4,128,128]{3,2,1,0:T(8,128)(2,1)} %get-tuple-element.189) | copy-start | bytes 1572868 | tf_op jit(solution)/shard_map/while
  247.5 3.5 %copy-start.2 = (bf16[4,4,768,128]{3,2,1,0:T(8,128)(2,1)S(1)}, bf16[4,4,768,128]{3,2,1,0:T(8,128)(2,1)}, u32[]{:S(2)}) copy-start(bf16[4,4,768,128]{3,2,1,0:T(8,128)(2,1)} %get-tuple-element.188) | copy-start | bytes 9437188 | tf_op jit(solution)/shard_map/while
  253.7 1.9 copy-start.3
  255.6 2.4 copy-start.4
  264.0 3.0 %copy-start.1 = (bf16[4,4,768,128]{3,2,1,0:T(8,128)(2,1)S(1)}, bf16[4,4,768,128]{3,2,1,0:T(8,128)(2,1)}, u32[]{:S(2)}) copy-start(bf16[4,4,768,128]{3,2,1,0:T(8,128)(2,1)} %get-tuple-element.186) | copy-start | bytes 9437188 | tf_op jit(solution)/shard_map/while
  264.1 3.0 %copy-start.5 = (bf16[4,4,128,128]{3,2,1,0:T(8,128)(2,1)S(1)}, bf16[4,4,128,128]{3,2,1,0:T(8,128)(2,1)}, u32[]{:S(2)}) copy-start(bf16[4,4,128,128]{3,2,1,0:T(8,128)(2,1)} %get-tuple-element.189) | copy-start | bytes 1572868 | tf_op jit(solution)/shard_map/while
  264.1 3.5 %copy-start.2 = (bf16[4,4,768,128]{3,2,1,0:T(8,128)(2,1)S(1)}, bf16[4,4,768,128]{3,2,1,0:T(8,128)(2,1)}, u32[]{:S(2)}) copy-start(bf16[4,4,768,128]{3,2,1,0:T(8,128)(2,1)} %get-tuple-element.188) | copy-start | bytes 9437188 | tf_op jit(solution)/shard_map/while
  270.2 1.9 copy-start.3
  272.1 2.4 copy-start.4
Sparse Core Ops, SparseCore 0:
  12.1 173.6 all-gather.2
